TPU v7x, 32 devices: a whole 2x2x4 slice. The times are simulated.
32 devices in a mesh: wave: 8 (over z, y), lev: 4 (over x, core).
Axes of the slice: x: 2, y: 2, z: 4, core: 2. Of those that a mesh axis runs over, the one named last changes fastest.
Arguments:
- spectral: float32 [8, 136, 2, 1280], P('wave', 'lev'), may hold values from -6 to 6
- to_modes: float32 [136, 136], replicated
- from_modes: float32 [136, 136], replicated
- mode_depths: float32 [136], replicated, may hold values from 0.05 to 5
- legendre: float32 [8, 16, 1280], P('wave'), may hold values from -0.03125 to 0.03125
- wave_ids: int32 [8], replicated, may hold values from 0 to 1279, as said below
- lat_points: int32 [16], P('wave'), may hold values from 20 to 5136, as said below
Outputs:
- grid: float32 [136, 16, 5136], P('lev', 'wave')
Inputs may be any that keep to these rules, and one draw needn't show every extreme that they name: `wave_ids`: distinct and ascending; 0 and 1279 are always among them. `lat_points`: each is 20 + 4 k for a whole k; not falling along the latitudes; the last is always 5136.
All inputs are finite; a program needn't handle non-finite values.
Results may differ from a plain program's by a relative error of at most 0.0003.
Values sent between devices are 32-bit elements; how exact they have to be, the bound alone decides.
No kernel may reach another device: no remote copies, remote signals or barrier semaphores. Data moves between devices by JAX's collectives and lax.ppermute only.
A program may use at most 64 MiB of HBM per device.

v0:
```python
import math
import jax
import jax.numpy as jnp
from jax import lax
from jax.sharding import PartitionSpec as P

LONS = 5136
two_pi = 2.0 * math.pi


def on_device(spectral, to_modes, from_modes, mode_depths, legendre, wave_ids, lat_points):
    highest = lax.Precision.HIGHEST
    waves_here = spectral.shape[0]
    total_orders = spectral.shape[3]
    block_len = total_orders // lax.axis_size("lev")
    columns = lax.all_to_all(spectral, "lev", split_axis=3, concat_axis=1, tiled=True)
    mode_coeffs = jnp.einsum("kl,wlcn->wkcn", to_modes, columns, precision=highest)
    first_order = lax.axis_index("lev") * block_len
    order_ids = first_order + jnp.arange(block_len)
    orders = order_ids.astype(jnp.float32)
    damping = 1.0 + mode_depths[:, None] * (orders * (orders + 1.0))[None, :] / float(
        total_orders * total_orders
    )
    divergence = jnp.einsum(
        "lk,wkcn->wlcn", from_modes, mode_coeffs / damping[None, :, None, :], precision=highest
    )
    own_ids = lax.dynamic_slice_in_dim(wave_ids, lax.axis_index("wave") * waves_here, waves_here)
    level_major = lax.all_to_all(divergence, "lev", split_axis=1, concat_axis=3, tiled=True)
    keep_mask = (jnp.arange(total_orders)[None, :] >= own_ids[:, None]).astype(jnp.float32)
    fourier = jnp.einsum(
        "wjn,wlcn->lwcj", legendre * keep_mask[:, None, :], level_major, precision=highest
    )
    band_data = lax.all_to_all(fourier, "wave", split_axis=3, concat_axis=1, tiled=True)
    positions = jnp.arange(LONS)

    def one_row(inputs):
        coeffs, points = inputs
        residue = wave_ids[:, None] * positions[None, :] % points
        phases = jnp.float32(two_pi) * residue.astype(jnp.float32) / points.astype(jnp.float32)
        weight = jnp.where(2 * wave_ids < points, jnp.where(wave_ids == 0, 1.0, 2.0), 0.0).astype(
            jnp.float32
        )
        basis_table = jnp.concatenate(
            [jnp.cos(phases) * weight[:, None], jnp.sin(phases) * weight[:, None]], 0
        )
        coefficient = jnp.concatenate([coeffs[:, :, 0], -coeffs[:, :, 1]], 1)
        lat_row = jnp.dot(coefficient, basis_table, precision=highest)
        return lat_row * (positions < points).astype(jnp.float32)[None, :]

    lat_rows = lax.map(one_row, (jnp.moveaxis(band_data, 3, 0), lat_points))
    return jnp.transpose(lat_rows, (1, 0, 2))


def solution(mesh):
    return jax.shard_map(
        on_device,
        mesh=mesh,
        in_specs=(
            P("wave", "lev", None, None),
            P(),
            P(),
            P(),
            P("wave", None, None),
            P(),
            P("wave"),
        ),
        out_specs=P("lev", "wave", None),
        check_vma=False,
    )
```

profile of v0, /device:TPU:0, one launch (start us, length us, event | category | flops | bytes accessed | tf_op | source)
XLA Modules:
  0.0 79.2 jit_solution(634367973494513038)
XLA Ops:
  0.0 0.0 copy-start
  0.0 2.6 %copy.29 = f32[1,34,2,1280]{1,2,0,3:T(2,128)S(1)} copy(f32[1,34,2,1280]{3,2,1,0:T(2,128)} %param.9) | data formatting | bytes 696320 | tf_op args[0]
  2.6 0.0 copy-start.4
  2.7 3.0 %reshape.90 = f32[4,1,21760]{2,1,0:T(1,128)} reshape(f32[1280,1,2,34]{3,2,1,0:T(2,128)S(1)} %bitcast.71) | data formatting | bytes 696320
  5.7 4.2 %all-to-all-start = ((f32[4,1,21760]{2,1,0:T(1,128)}), f32[4,1,21760]{2,1,0:T(1,128)S(1)}, u32[]{:S(2)}, u32[]{:S(2)}) async-start(f32[4,1,21760]{2,1,0:T(1,128)} %reshape.90), calls=%async_computation | async-start | bytes 696320 | tf_op jit(solution)/shard_map/all_to_all | solution.py:16
  9.9 0.0 copy-done.4
  9.9 0.1 multiply_add_fusion
  10.0 6.9 %all-to-all-done = f32[4,1,21760]{2,1,0:T(1,128)S(1)} async-done(((f32[4,1,21760]{2,1,0:T(1,128)}), f32[4,1,21760]{2,1,0:T(1,128)S(1)}, u32[]{:S(2)}, u32[]{:S(2)}) %all-to-all-start) | async-done | bytes 348192 | tf_op jit(solution)/shard_map/all_to_all | solution.py:16
  16.9 0.5 broadcast.99
  17.4 1.6 %reduce = f32[4,21760]{1,0:T(4,128)S(1)} reduce(f32[4,1,21760]{2,1,0:T(1,128)S(1)} %all-to-all-done, f32[]{:T(128)} %broadcast.99), dimensions={1}, to_apply=%all_to_all.35.reduce_sub_computation | reduce | bytes 696324 | tf_op jit(solution)/shard_map/all_to_all | solution.py:16
  19.0 2.2 %reshape.91 = f32[1280,1,2,34]{3,2,1,0:T(2,128)S(1)} reshape(f32[4,21760]{1,0:T(4,128)S(1)} %reduce) | data formatting | bytes 696320
  21.3 0.0 copy-start.1
  21.3 1.3 %copy.30 = f32[1,34,2,4,320]{4,2,1,3,0:T(2,128)S(1)} copy(f32[1,34,2,4,320]{1,2,4,3,0:T(2,128)S(1)} %bitcast.70) | data formatting | bytes 696320 | tf_op jit(solution)/shard_map/all_to_all | solution.py:16
  22.5 0.0 copy-done
  22.6 0.5 fusion.21
  23.1 0.0 copy-done.1
  23.1 0.0 copy-start.3
  23.1 0.5 convolution_bitcast_fusion
  23.6 1.0 %copy.32 = f32[1,136,2,320]{3,2,0,1:T(2,128)} copy(f32[1,136,2,320]{3,1,2,0:T(8,128)S(1)} %convolution_bitcast_fusion) | data formatting | bytes 696320 | tf_op jit(solution)/shard_map/lk,wkcn->wlcn/transpose | solution.py:24
  24.6 0.0 copy-start.2
  24.6 0.0 copy-start.6
  24.6 3.6 %all-to-all-start.1 = ((f32[1,136,2,320]{3,2,0,1:T(2,128)}), f32[1,136,2,320]{3,2,0,1:T(2,128)S(1)}, u32[]{:S(2)}, u32[]{:S(2)}) async-start(f32[1,136,2,320]{3,2,0,1:T(2,128)} %copy.32), calls=%async_computation.1 | async-start | bytes 835584 | tf_op jit(solution)/shard_map/all_to_all | solution.py:28
  28.2 0.0 copy-done.3
  28.2 0.7 dynamic_slice.11
  28.9 0.6 fusion.28
  29.5 6.4 %all-to-all-done.1 = f32[1,136,2,320]{3,2,0,1:T(2,128)S(1)} async-done(((f32[1,136,2,320]{3,2,0,1:T(2,128)}), f32[1,136,2,320]{3,2,0,1:T(2,128)S(1)}, u32[]{:S(2)}, u32[]{:S(2)}) %all-to-all-start.1) | async-done | bytes 348192 | tf_op jit(solution)/shard_map/all_to_all | solution.py:28
  35.9 0.1 copy.38
  36.0 0.3 reshape.89
  36.3 0.0 copy-done.2
  36.3 0.8 convolution_bitcast_fusion.2
  37.1 0.7 reshape.92
  37.8 6.5 %all-to-all-start.2 = ((f32[8,1,136]{2,1,0:T(1,128)}), f32[8,1,136]{2,1,0:T(1,128)S(1)}, u32[]{:S(2)}, u32[]{:S(2)}) async-start(f32[8,1,136]{2,1,0:T(1,128)} %reshape.92), calls=%async_computation.2 | async-start | bytes 16384 | tf_op jit(solution)/shard_map/all_to_all | solution.py:33
  44.3 6.5 %all-to-all-done.2 = f32[8,1,136]{2,1,0:T(1,128)S(1)} async-done(((f32[8,1,136]{2,1,0:T(1,128)}), f32[8,1,136]{2,1,0:T(1,128)S(1)}, u32[]{:S(2)}, u32[]{:S(2)}) %all-to-all-start.2) | async-done | bytes 4384 | tf_op jit(solution)/shard_map/all_to_all | solution.py:33
  50.8 0.7 reduce.1
  51.5 0.1 reshape.93
  51.6 0.0 copy-done.6
  51.6 26.6 %while.12 = (s32[]{:T(128)}, f32[2,34,5136]{2,0,1:T(2,128)S(1)}, f32[2,34,8,2]{1,2,3,0:T(8,128)S(1)}, s32[8]{0:T(128)S(1)}, s32[2]{0:T(128)S(1)}, /*index=5*/s32[]{:T(128)}, s32[]{:T(128)}) while((s32[]{:T(128)}, f32[2,34,5136]{2,0,1:T(2,128)S(1)}, f32[2,34,8,2]{1,2,3,0:T(8,128)S(1)}, s32[8]{0:T(128)S(1)}, ...), condition=%wide.region_1.2_spmd.clone.clone, body=%wide.region_0.1_spmd.clone.clone.sunk | while | flops 34329884 | bytes 4202137 | solution.py:50
  51.6 0.6 dynamic_slice.20
  53.5 0.6 compare_select_fusion.3
  54.8 2.3 %cosine_multiply_fusion.2 = (f32[8,5136]{1,0:T(8,128)S(1)}, f32[8,5136]{1,0:T(8,128)S(1)}) fusion(f32[8]{0:T(128)S(1)} %compare_select_fusion.3, f32[]{:T(128)S(6)} %convert_element_type.54, pred[]{:T(512)S(6)} %lt.78, s32[]{:T(128)S(6)} %select_n.59, s32[8]{0:T(128)S(1)} %get-tuple-element.139), kind=kLoop, calls=%fused_computation.15.clone.1 | loop fusion | flops 534144 | bytes 328777 | tf_op jit(solution)/shard_map/while/body/eval_jaxpr/mul | solution.py:44
  57.1 0.7 fusion.37
  57.8 0.9 %fusion.38 = f32[1,34,5136]{2,1,0:T(8,128)S(1)} fusion(f32[5136]{0:T(1024)S(1)} %fusion.37, f32[8,5136]{1,0:T(8,128)S(1)} %get-tuple-element.118, f32[8,5136]{1,0:T(8,128)S(1)} %get-tuple-element.119, f32[34,8]{0,1:T(8,128)S(1)} %get-tuple-element.120, f32[34,8]{0,1:T(8,128)S(1)} %get-tuple-element.121), kind=kOutput, calls=%fused_computation.2.clone.1 | convolution fusion | flops 33785152 | bytes 1049920 | tf_op jit(solution)/shard_map/while/body/eval_jaxpr/dot_general | solution.py:47
  58.7 0.7 copy.49
  59.4 5.3 %dynamic_update_slice.7 = f32[2,34,5136]{2,0,1:T(2,128)S(1)} dynamic-update-slice(f32[2,34,5136]{2,0,1:T(2,128)S(1)} %get-tuple-element.130, f32[1,34,5136]{2,0,1:T(1,128)S(1)} %copy.49, s32[]{:T(128)} %get-tuple-element.129, s32[]{:T(128)} %constant.25.clone.1..sunk, s32[]{:T(128)} %constant.25.clone.1..sunk) | dynamic-update-slice | bytes 1396996 | tf_op jit(solution)/shard_map/while/body/jit(dynamic_update_index_in_dim)/dynamic_update_slice | solution.py:50
  64.8 0.6 dynamic_slice.20
  66.7 0.6 compare_select_fusion.3
  68.0 2.3 %cosine_multiply_fusion.2 = (f32[8,5136]{1,0:T(8,128)S(1)}, f32[8,5136]{1,0:T(8,128)S(1)}) fusion(f32[8]{0:T(128)S(1)} %compare_select_fusion.3, f32[]{:T(128)S(6)} %convert_element_type.54, pred[]{:T(512)S(6)} %lt.78, s32[]{:T(128)S(6)} %select_n.59, s32[8]{0:T(128)S(1)} %get-tuple-element.139), kind=kLoop, calls=%fused_computation.15.clone.1 | loop fusion | flops 534144 | bytes 328777 | tf_op jit(solution)/shard_map/while/body/eval_jaxpr/mul | solution.py:44
  70.3 0.7 fusion.37
  71.0 0.9 %fusion.38 = f32[1,34,5136]{2,1,0:T(8,128)S(1)} fusion(f32[5136]{0:T(1024)S(1)} %fusion.37, f32[8,5136]{1,0:T(8,128)S(1)} %get-tuple-element.118, f32[8,5136]{1,0:T(8,128)S(1)} %get-tuple-element.119, f32[34,8]{0,1:T(8,128)S(1)} %get-tuple-element.120, f32[34,8]{0,1:T(8,128)S(1)} %get-tuple-element.121), kind=kOutput, calls=%fused_computation.2.clone.1 | convolution fusion | flops 33785152 | bytes 1049920 | tf_op jit(solution)/shard_map/while/body/eval_jaxpr/dot_general | solution.py:47
  71.9 0.7 copy.49
  72.6 5.5 %dynamic_update_slice.7 = f32[2,34,5136]{2,0,1:T(2,128)S(1)} dynamic-update-slice(f32[2,34,5136]{2,0,1:T(2,128)S(1)} %get-tuple-element.130, f32[1,34,5136]{2,0,1:T(1,128)S(1)} %copy.49, s32[]{:T(128)} %get-tuple-element.129, s32[]{:T(128)} %constant.25.clone.1..sunk, s32[]{:T(128)} %constant.25.clone.1..sunk) | dynamic-update-slice | bytes 1396996 | tf_op jit(solution)/shard_map/while/body/jit(dynamic_update_index_in_dim)/dynamic_update_slice | solution.py:50
  78.1 0.0 copy-start.5
  78.1 1.1 %copy-done.5 = f32[2,34,5136]{2,0,1:T(2,128)} copy-done((f32[2,34,5136]{2,0,1:T(2,128)}, f32[2,34,5136]{2,0,1:T(2,128)S(1)}, u32[]{:S(2)}) %copy-start.5) | copy-done | bytes 1397016
  (8 shorter events, 0.1 us)
Async XLA Ops:
  0.0 22.5 %copy-start = (f32[136,136]{1,0:T(8,128)S(1)}, f32[136,136]{1,0:T(8,128)}, u32[]{:S(2)}) copy-start(f32[136,136]{1,0:T(8,128)} %param.10) | copy-start | bytes 221956
  2.6 7.3 %copy-start.4 = (f32[136]{0:T(256)S(1)}, f32[136]{0:T(256)}, u32[]{:S(2)}) copy-start(f32[136]{0:T(256)} %param.12) | copy-start | bytes 1636
  5.7 11.2 %all-to-all-start = ((f32[4,1,21760]{2,1,0:T(1,128)}), f32[4,1,21760]{2,1,0:T(1,128)S(1)}, u32[]{:S(2)}, u32[]{:S(2)}) async-start(f32[4,1,21760]{2,1,0:T(1,128)} %reshape.90), calls=%async_computation | async-start | bytes 696320 | tf_op jit(solution)/shard_map/all_to_all | solution.py:16
  21.3 1.8 %copy-start.1 = (f32[136,136]{1,0:T(8,128)S(1)}, f32[136,136]{1,0:T(8,128)}, u32[]{:S(2)}) copy-start(f32[136,136]{1,0:T(8,128)} %param.11) | copy-start | bytes 221956
  23.1 5.1 %copy-start.3 = (s32[8]{0:T(128)S(1)}, s32[8]{0:T(128)}, u32[]{:S(2)}) copy-start(s32[8]{0:T(128)} %param.14) | copy-start | bytes 100
  24.6 11.7 %copy-start.2 = (f32[1,16,1280]{2,1,0:T(8,128)S(1)}, f32[1,16,1280]{2,1,0:T(8,128)}, u32[]{:S(2)}) copy-start(f32[1,16,1280]{2,1,0:T(8,128)} %param.13) | copy-start | bytes 245764
  24.6 27.0 %copy-start.6 = (s32[2]{0:T(128)S(1)}, s32[2]{0:T(128)}, u32[]{:S(2)}) copy-start(s32[2]{0:T(128)} %param.15) | copy-start | bytes 28
  24.6 11.3 %all-to-all-start.1 = ((f32[1,136,2,320]{3,2,0,1:T(2,128)}), f32[1,136,2,320]{3,2,0,1:T(2,128)S(1)}, u32[]{:S(2)}, u32[]{:S(2)}) async-start(f32[1,136,2,320]{3,2,0,1:T(2,128)} %copy.32), calls=%async_computation.1 | async-start | bytes 835584 | tf_op jit(solution)/shard_map/all_to_all | solution.py:28
  37.8 13.0 %all-to-all-start.2 = ((f32[8,1,136]{2,1,0:T(1,128)}), f32[8,1,136]{2,1,0:T(1,128)S(1)}, u32[]{:S(2)}, u32[]{:S(2)}) async-start(f32[8,1,136]{2,1,0:T(1,128)} %reshape.92), calls=%async_computation.2 | async-start | bytes 16384 | tf_op jit(solution)/shard_map/all_to_all | solution.py:33
  78.1 1.1 %copy-start.5 = (f32[2,34,5136]{2,0,1:T(2,128)}, f32[2,34,5136]{2,0,1:T(2,128)S(1)}, u32[]{:S(2)}) copy-start(f32[2,34,5136]{2,0,1:T(2,128)S(1)} %get-tuple-element.40) | copy-start | bytes 4190980
where the time goes:
time: 79.7 us; the launch traced here: 79.2 us
  local copies, waits for them, and re-layouts  27.1 us (34%)
  waiting for transfers between devices  19.7 us (25%)
  starting transfers between devices  14.3 us (18%)
  other arithmetic  10.3 us (13%)
  loops' own time  4.04 us (5%)
  matrix products  3.55 us (4%)
    dynamic_update_slice x4, local copies, waits for them, and re-layouts, on_device(): lat_rows = lax.map(one_row, (jnp.moveaxis(band_data, 3, 0), lat_points))  12.3 us
    unnamed x19, local copies, waits for them, and re-layouts  9.8 us
    all_to_all x1, waiting for transfers between devices, on_device(): lax.all_to_all(spectral, 'lev', split_axis=3, concat_axis=1, tiled=True)  6.85 us
    all_to_all x1, waiting for transfers between devices, on_device(): lax.all_to_all(fourier, 'wave', split_axis=3, concat_axis=1, tiled=True)  6.51 us
    all_to_all x1, starting transfers between devices, on_device(): lax.all_to_all(fourier, 'wave', split_axis=3, concat_axis=1, tiled=True)  6.5 us
    all_to_all x1, waiting for transfers between devices, on_device(): lax.all_to_all(divergence, 'lev', split_axis=1, concat_axis=3, tiled=True)  6.37 us
    mul x2, other arithmetic, one_row(): jnp.cos(phases) * weight[:, None]  4.69 us
    all_to_all x1, starting transfers between devices, on_device(): lax.all_to_all(spectral, 'lev', split_axis=3, concat_axis=1, tiled=True)  4.21 us
  transfers between devices with their start and end apart: 3, of which 3 were waited for; matrix products, arithmetic and copies ran while one was open for 2% of the time, Pallas kernels for 0%

commit v1 on v0

--- a/solution.py
+++ b/solution.py
@@ -1,3 +1,4 @@
+import functools
 import math
 import jax
 import jax.numpy as jnp
@@ -8,12 +9,23 @@
 two_pi = 2.0 * math.pi
 
 
+def raise_page(payload, pos_dim, axis_no, dev_axis):
+    r2 = lax.psum(1, axis_name=dev_axis)
+    all_values = jnp.stack(jnp.split(payload, r2, axis=axis_no), axis=0)
+    taken_in = lax.all_to_all(all_values, axis_name=dev_axis, split_axis=0, concat_axis=0)
+    arr_now = jnp.concatenate(taken_in, axis=pos_dim)
+    return arr_now
+
+
+guide_tails = functools.partial(raise_page, pos_dim=1, axis_no=3, dev_axis="lev")
+
+
 def on_device(spectral, to_modes, from_modes, mode_depths, legendre, wave_ids, lat_points):
     highest = lax.Precision.HIGHEST
     waves_here = spectral.shape[0]
     total_orders = spectral.shape[3]
     block_len = total_orders // lax.axis_size("lev")
-    columns = lax.all_to_all(spectral, "lev", split_axis=3, concat_axis=1, tiled=True)
+    columns = guide_tails(spectral)
     mode_coeffs = jnp.einsum("kl,wlcn->wkcn", to_modes, columns, precision=highest)
     first_order = lax.axis_index("lev") * block_len
     order_ids = first_order + jnp.arange(block_len)

time: 79.7 us -> 72.1 us (0.905)
  local copies, waits for them, and re-layouts: 27.1 us -> 19.3 us
  waiting for transfers between devices: 19.7 us -> 20.5 us
    unnamed x19 -> x16, local copies, waits for them, and re-layouts: 9.8 us -> 1.89 us
    all_to_all x2 -> x0, local copies, waits for them, and re-layouts: 1.79 us -> none  [on_device(): lax.all_to_all(spectral, 'lev', split_axis=3, concat_axis=1, tiled=True)]
    all_to_all x1 -> x0, other arithmetic: 1.62 us -> none  [on_device(): lax.all_to_all(spectral, 'lev', split_axis=3, concat_axis=1, tiled=True)]
    another operation x2 -> x3, local copies, waits for them, and re-layouts: 0.4 us -> 1.79 us  [the longest x1 1.4 us: raise_page(): all_values = jnp.stack(jnp.split(payload, r2, axis=axis_no), axis=0)]
    another operation x0 -> x1, other arithmetic: none -> 0.95 us  [raise_page(): all_values = jnp.stack(jnp.split(payload, r2, axis=axis_no), axis=0)]
where the time goes in v1:
time: 72.1 us; the launch traced here: 71.6 us
  waiting for transfers between devices  20.5 us (28%)
  local copies, waits for them, and re-layouts  19.3 us (27%)
  starting transfers between devices  14.4 us (20%)
  other arithmetic  9.65 us (13%)
  loops' own time  4.04 us (6%)
  matrix products  3.55 us (5%)
    dynamic_update_slice x4, local copies, waits for them, and re-layouts, on_device(): lat_rows = lax.map(one_row, (jnp.moveaxis(band_data, 3, 0), lat_points))  12.3 us
    all_to_all x1, waiting for transfers between devices, raise_page(): lax.all_to_all(all_values, axis_name=dev_axis, split_axis=0, concat_axis=0)  7.6 us
    all_to_all x1, waiting for transfers between devices, on_device(): lax.all_to_all(fourier, 'wave', split_axis=3, concat_axis=1, tiled=True)  6.51 us
    all_to_all x1, starting transfers between devices, on_device(): lax.all_to_all(fourier, 'wave', split_axis=3, concat_axis=1, tiled=True)  6.51 us
    all_to_all x1, waiting for transfers between devices, on_device(): lax.all_to_all(divergence, 'lev', split_axis=1, concat_axis=3, tiled=True)  6.4 us
    mul x2, other arithmetic, one_row(): jnp.cos(phases) * weight[:, None]  4.69 us
    all_to_all x1, starting transfers between devices, raise_page(): lax.all_to_all(all_values, axis_name=dev_axis, split_axis=0, concat_axis=0)  4.34 us
    another operation x1, loops' own time, on_device(): lat_rows = lax.map(one_row, (jnp.moveaxis(band_data, 3, 0), lat_points))  4.04 us
  transfers between devices with their start and end apart: 3, of which 3 were waited for; matrix products, arithmetic and copies ran while one was open for 2% of the time, Pallas kernels for 0%

profile of v1, /device:TPU:0, one launch (start us, length us, event | category | flops | bytes accessed | tf_op | source)
XLA Modules:
  0.0 71.6 jit_solution(1712684438005486869)
XLA Ops:
  0.0 0.0 copy-start
  0.0 0.0 copy-start.4
  0.0 1.4 %slice_bitcast_fusion.4 = (f32[1,1,34,2,320]{4,3,2,1,0:T(2,128)S(1)}, f32[1,1,34,2,320]{4,3,2,1,0:T(2,128)S(1)}, f32[1,1,34,2,320]{4,3,2,1,0:T(2,128)S(1)}, f32[1,1,34,2,320]{4,3,2,1,0:T(2,128)S(1)}) fusion(f32[1,34,2,1280]{3,2,1,0:T(2,128)} %param.9), kind=kLoop, calls=%fused_computation.43 | loop fusion | bytes 696320 | tf_op jit(solution)/shard_map/stack | solution.py:14
  1.4 1.0 %pad_maximum_fusion = f32[4,1,34,2,320]{4,3,2,1,0:T(2,128)} fusion(f32[1,1,34,2,320]{4,3,2,1,0:T(2,128)S(1)} %get-tuple-element.85, f32[1,1,34,2,320]{4,3,2,1,0:T(2,128)S(1)} %get-tuple-element.86, f32[1,1,34,2,320]{4,3,2,1,0:T(2,128)S(1)} %get-tuple-element.84, f32[1,1,34,2,320]{4,3,2,1,0:T(2,128)S(1)} %get-tuple-element.83), kind=kLoop, calls=%fused_computation.35 | loop fusion | flops 261120 | bytes 696320 | tf_op jit(solution)/shard_map/stack | solution.py:14
  2.4 0.0 copy-start.1
  2.4 4.3 %all-to-all-start = ((f32[4,1,34,2,320]{4,3,2,1,0:T(2,128)}), f32[4,1,34,2,320]{4,3,2,1,0:T(2,128)S(1)}, u32[]{:S(2)}, u32[]{:S(2)}) async-start(f32[4,1,34,2,320]{4,3,2,1,0:T(2,128)} %pad_maximum_fusion), calls=%async_computation | async-start | bytes 835584 | tf_op jit(solution)/shard_map/all_to_all | solution.py:15
  6.7 0.0 copy-done.4
  6.7 0.1 multiply_add_fusion
  6.8 7.6 %all-to-all-done = f32[4,1,34,2,320]{4,3,2,1,0:T(2,128)S(1)} async-done(((f32[4,1,34,2,320]{4,3,2,1,0:T(2,128)}), f32[4,1,34,2,320]{4,3,2,1,0:T(2,128)S(1)}, u32[]{:S(2)}, u32[]{:S(2)}) %all-to-all-start) | async-done | bytes 348192 | tf_op jit(solution)/shard_map/all_to_all | solution.py:15
  14.4 0.0 copy-done
  14.4 0.5 fusion.21
  14.9 0.0 copy-done.1
  15.0 0.0 copy-start.3
  15.0 0.5 convolution_bitcast_fusion
  15.5 1.0 %copy.20 = f32[1,136,2,320]{3,2,0,1:T(2,128)} copy(f32[1,136,2,320]{3,1,2,0:T(8,128)S(1)} %convolution_bitcast_fusion) | data formatting | bytes 696320 | tf_op jit(solution)/shard_map/lk,wkcn->wlcn/transpose | solution.py:36
  16.5 0.0 copy-start.2
  16.5 0.0 copy-start.6
  16.5 3.6 %all-to-all-start.1 = ((f32[1,136,2,320]{3,2,0,1:T(2,128)}), f32[1,136,2,320]{3,2,0,1:T(2,128)S(1)}, u32[]{:S(2)}, u32[]{:S(2)}) async-start(f32[1,136,2,320]{3,2,0,1:T(2,128)} %copy.20), calls=%async_computation.1 | async-start | bytes 835584 | tf_op jit(solution)/shard_map/all_to_all | solution.py:40
  20.1 0.0 copy-done.3
  20.1 0.6 dynamic_slice.11
  20.7 0.6 fusion.28
  21.3 6.4 %all-to-all-done.1 = f32[1,136,2,320]{3,2,0,1:T(2,128)S(1)} async-done(((f32[1,136,2,320]{3,2,0,1:T(2,128)}), f32[1,136,2,320]{3,2,0,1:T(2,128)S(1)}, u32[]{:S(2)}, u32[]{:S(2)}) %all-to-all-start.1) | async-done | bytes 348192 | tf_op jit(solution)/shard_map/all_to_all | solution.py:40
  27.7 0.1 copy.26
  27.8 0.3 reshape.90
  28.1 0.0 copy-done.2
  28.1 0.8 %convolution_bitcast_fusion.2 = f32[34,1,2,16]{0,3,2,1:T(8,128)S(1)} fusion(f32[34,2,1280]{2,0,1:T(8,128)S(1)} %reshape.90, f32[1,16,1280]{2,1,0:T(8,128)S(1)} %copy-done.2, f32[1280]{0:T(1024)S(1)} %fusion.28), kind=kOutput, calls=%fused_computation.32 | convolution fusion | flops 16732160 | bytes 439552 | tf_op jit(solution)/shard_map/wjn,wlcn->lwcj/dot_general | solution.py:42
  29.0 0.7 reshape.91
  29.6 6.5 %all-to-all-start.2 = ((f32[8,1,136]{2,1,0:T(1,128)}), f32[8,1,136]{2,1,0:T(1,128)S(1)}, u32[]{:S(2)}, u32[]{:S(2)}) async-start(f32[8,1,136]{2,1,0:T(1,128)} %reshape.91), calls=%async_computation.2 | async-start | bytes 16384 | tf_op jit(solution)/shard_map/all_to_all | solution.py:45
  36.2 6.5 %all-to-all-done.2 = f32[8,1,136]{2,1,0:T(1,128)S(1)} async-done(((f32[8,1,136]{2,1,0:T(1,128)}), f32[8,1,136]{2,1,0:T(1,128)S(1)}, u32[]{:S(2)}, u32[]{:S(2)}) %all-to-all-start.2) | async-done | bytes 4384 | tf_op jit(solution)/shard_map/all_to_all | solution.py:45
  42.7 0.5 broadcast.99
  43.2 0.7 reduce
  43.9 0.1 reshape.92
  44.0 0.0 copy-done.6
  44.0 26.6 %while.12 = (s32[]{:T(128)}, f32[2,34,5136]{2,0,1:T(2,128)S(1)}, f32[2,34,8,2]{1,2,3,0:T(8,128)S(1)}, s32[8]{0:T(128)S(1)}, s32[2]{0:T(128)S(1)}, /*index=5*/s32[]{:T(128)}, s32[]{:T(128)}) while((s32[]{:T(128)}, f32[2,34,5136]{2,0,1:T(2,128)S(1)}, f32[2,34,8,2]{1,2,3,0:T(8,128)S(1)}, s32[8]{0:T(128)S(1)}, ...), condition=%wide.region_1.2_spmd.clone.clone, body=%wide.region_0.1_spmd.clone.clone.sunk | while | flops 34329884 | bytes 4202137 | solution.py:62
  44.0 0.6 dynamic_slice.20
  45.9 0.6 compare_select_fusion.3
  47.2 2.3 %cosine_multiply_fusion.2 = (f32[8,5136]{1,0:T(8,128)S(1)}, f32[8,5136]{1,0:T(8,128)S(1)}) fusion(f32[8]{0:T(128)S(1)} %compare_select_fusion.3, f32[]{:T(128)S(6)} %convert_element_type.54, pred[]{:T(512)S(6)} %lt.78, s32[]{:T(128)S(6)} %select_n.59, s32[8]{0:T(128)S(1)} %get-tuple-element.143), kind=kLoop, calls=%fused_computation.15.clone.1 | loop fusion | flops 534144 | bytes 328777 | tf_op jit(solution)/shard_map/while/body/eval_jaxpr/mul | solution.py:56
  49.5 0.7 fusion.37
  50.2 0.9 %fusion.38 = f32[1,34,5136]{2,1,0:T(8,128)S(1)} fusion(f32[5136]{0:T(1024)S(1)} %fusion.37, f32[8,5136]{1,0:T(8,128)S(1)} %get-tuple-element.122, f32[8,5136]{1,0:T(8,128)S(1)} %get-tuple-element.123, f32[34,8]{0,1:T(8,128)S(1)} %get-tuple-element.124, f32[34,8]{0,1:T(8,128)S(1)} %get-tuple-element.125), kind=kOutput, calls=%fused_computation.2.clone.1 | convolution fusion | flops 33785152 | bytes 1049920 | tf_op jit(solution)/shard_map/while/body/eval_jaxpr/dot_general | solution.py:59
  51.1 0.7 %copy.37 = f32[1,34,5136]{2,0,1:T(1,128)S(1)} copy(f32[1,34,5136]{2,1,0:T(8,128)S(1)} %fusion.38) | data formatting | bytes 1396992 | tf_op jit(solution)/shard_map/while/body/jit(dynamic_update_index_in_dim)/dynamic_update_slice | solution.py:62
  51.8 5.3 %dynamic_update_slice.7 = f32[2,34,5136]{2,0,1:T(2,128)S(1)} dynamic-update-slice(f32[2,34,5136]{2,0,1:T(2,128)S(1)} %get-tuple-element.134, f32[1,34,5136]{2,0,1:T(1,128)S(1)} %copy.37, s32[]{:T(128)} %get-tuple-element.133, s32[]{:T(128)} %constant.25.clone.1..sunk, s32[]{:T(128)} %constant.25.clone.1..sunk) | dynamic-update-slice | bytes 1396996 | tf_op jit(solution)/shard_map/while/body/jit(dynamic_update_index_in_dim)/dynamic_update_slice | solution.py:62
  57.2 0.6 dynamic_slice.20
  59.1 0.6 compare_select_fusion.3
  60.4 2.3 %cosine_multiply_fusion.2 = (f32[8,5136]{1,0:T(8,128)S(1)}, f32[8,5136]{1,0:T(8,128)S(1)}) fusion(f32[8]{0:T(128)S(1)} %compare_select_fusion.3, f32[]{:T(128)S(6)} %convert_element_type.54, pred[]{:T(512)S(6)} %lt.78, s32[]{:T(128)S(6)} %select_n.59, s32[8]{0:T(128)S(1)} %get-tuple-element.143), kind=kLoop, calls=%fused_computation.15.clone.1 | loop fusion | flops 534144 | bytes 328777 | tf_op jit(solution)/shard_map/while/body/eval_jaxpr/mul | solution.py:56
  62.7 0.7 fusion.37
  63.4 0.9 %fusion.38 = f32[1,34,5136]{2,1,0:T(8,128)S(1)} fusion(f32[5136]{0:T(1024)S(1)} %fusion.37, f32[8,5136]{1,0:T(8,128)S(1)} %get-tuple-element.122, f32[8,5136]{1,0:T(8,128)S(1)} %get-tuple-element.123, f32[34,8]{0,1:T(8,128)S(1)} %get-tuple-element.124, f32[34,8]{0,1:T(8,128)S(1)} %get-tuple-element.125), kind=kOutput, calls=%fused_computation.2.clone.1 | convolution fusion | flops 33785152 | bytes 1049920 | tf_op jit(solution)/shard_map/while/body/eval_jaxpr/dot_general | solution.py:59
  64.3 0.7 %copy.37 = f32[1,34,5136]{2,0,1:T(1,128)S(1)} copy(f32[1,34,5136]{2,1,0:T(8,128)S(1)} %fusion.38) | data formatting | bytes 1396992 | tf_op jit(solution)/shard_map/while/body/jit(dynamic_update_index_in_dim)/dynamic_update_slice | solution.py:62
  65.0 5.5 %dynamic_update_slice.7 = f32[2,34,5136]{2,0,1:T(2,128)S(1)} dynamic-update-slice(f32[2,34,5136]{2,0,1:T(2,128)S(1)} %get-tuple-element.134, f32[1,34,5136]{2,0,1:T(1,128)S(1)} %copy.37, s32[]{:T(128)} %get-tuple-element.133, s32[]{:T(128)} %constant.25.clone.1..sunk, s32[]{:T(128)} %constant.25.clone.1..sunk) | dynamic-update-slice | bytes 1396996 | tf_op jit(solution)/shard_map/while/body/jit(dynamic_update_index_in_dim)/dynamic_update_slice | solution.py:62
  70.5 0.0 copy-start.5
  70.5 1.1 %copy-done.5 = f32[2,34,5136]{2,0,1:T(2,128)} copy-done((f32[2,34,5136]{2,0,1:T(2,128)}, f32[2,34,5136]{2,0,1:T(2,128)S(1)}, u32[]{:S(2)}) %copy-start.5) | copy-done | bytes 1397016
  (8 shorter events, 0.1 us)
Async XLA Ops:
  0.0 14.4 %copy-start = (f32[136,136]{1,0:T(8,128)S(1)}, f32[136,136]{1,0:T(8,128)}, u32[]{:S(2)}) copy-start(f32[136,136]{1,0:T(8,128)} %param.10) | copy-start | bytes 221956
  0.0 6.7 %copy-start.4 = (f32[136]{0:T(256)S(1)}, f32[136]{0:T(256)}, u32[]{:S(2)}) copy-start(f32[136]{0:T(256)} %param.12) | copy-start | bytes 1636
  2.4 12.6 %copy-start.1 = (f32[136,136]{1,0:T(8,128)S(1)}, f32[136,136]{1,0:T(8,128)}, u32[]{:S(2)}) copy-start(f32[136,136]{1,0:T(8,128)} %param.11) | copy-start | bytes 221956
  2.4 12.0 %all-to-all-start = ((f32[4,1,34,2,320]{4,3,2,1,0:T(2,128)}), f32[4,1,34,2,320]{4,3,2,1,0:T(2,128)S(1)}, u32[]{:S(2)}, u32[]{:S(2)}) async-start(f32[4,1,34,2,320]{4,3,2,1,0:T(2,128)} %pad_maximum_fusion), calls=%async_computation | async-start | bytes 835584 | tf_op jit(solution)/shard_map/all_to_all | solution.py:15
  15.0 5.1 %copy-start.3 = (s32[8]{0:T(128)S(1)}, s32[8]{0:T(128)}, u32[]{:S(2)}) copy-start(s32[8]{0:T(128)} %param.14) | copy-start | bytes 100
  16.5 11.7 %copy-start.2 = (f32[1,16,1280]{2,1,0:T(8,128)S(1)}, f32[1,16,1280]{2,1,0:T(8,128)}, u32[]{:S(2)}) copy-start(f32[1,16,1280]{2,1,0:T(8,128)} %param.13) | copy-start | bytes 245764
  16.5 27.5 %copy-start.6 = (s32[2]{0:T(128)S(1)}, s32[2]{0:T(128)}, u32[]{:S(2)}) copy-start(s32[2]{0:T(128)} %param.15) | copy-start | bytes 28
  16.5 11.3 %all-to-all-start.1 = ((f32[1,136,2,320]{3,2,0,1:T(2,128)}), f32[1,136,2,320]{3,2,0,1:T(2,128)S(1)}, u32[]{:S(2)}, u32[]{:S(2)}) async-start(f32[1,136,2,320]{3,2,0,1:T(2,128)} %copy.20), calls=%async_computation.1 | async-start | bytes 835584 | tf_op jit(solution)/shard_map/all_to_all | solution.py:40
  29.6 13.0 %all-to-all-start.2 = ((f32[8,1,136]{2,1,0:T(1,128)}), f32[8,1,136]{2,1,0:T(1,128)S(1)}, u32[]{:S(2)}, u32[]{:S(2)}) async-start(f32[8,1,136]{2,1,0:T(1,128)} %reshape.91), calls=%async_computation.2 | async-start | bytes 16384 | tf_op jit(solution)/shard_map/all_to_all | solution.py:45
  70.5 1.1 %copy-start.5 = (f32[2,34,5136]{2,0,1:T(2,128)}, f32[2,34,5136]{2,0,1:T(2,128)S(1)}, u32[]{:S(2)}) copy-start(f32[2,34,5136]{2,0,1:T(2,128)S(1)} %get-tuple-element.40) | copy-start | bytes 4190980
